TPU v7x, 256 devices: a whole 4x4x8 slice. The times are simulated.
256 devices in a mesh: grp: 8 (over x, core), tile: 32 (over z, y).
Axes of the slice: x: 4, y: 4, z: 8, core: 2. Of those that a mesh axis runs over, the one named last changes fastest.
Arguments:
- tx_fields: bfloat16 [64, 32768], P(None, 'tile'), may hold values from -6 to 6
- rx_fields: bfloat16 [128, 32768], P(None, 'tile'), may hold values from -6 to 6
- layer_of_cell: int32 [32768], P('tile'), may hold values from 0 to 31
- layer_cond: float32 [32], replicated, may hold values from 0.05 to 5
- tx_of_row: int32 [2816], replicated, may hold values from 0 to 63
- rx_of_row: int32 [2816], replicated, may hold values from 0 to 127
- damping: float32 [2816], replicated, may hold values from 0.5 to 5
- panel_order: int32 [2816], replicated, may hold values from 0 to 2815, each once
Outputs:
- trailing: float32 [2816, 2816], P('grp', 'tile')
- factor: float32 [2816, 1024], P('grp')
Inputs may be any that keep to these rules, and one draw needn't show every extreme that they name: `panel_order`: each data row appears exactly once; panel k is entries k * 512 to (k + 1) * 512 - 1.
All inputs are finite; a program needn't handle non-finite values.
Results may differ from a plain program's by a relative error of at most 0.0014.
Values may be sent and summed in bfloat16 or wider, within the bound.
A program may use at most 64 MiB of HBM per device.

v0:
```python
import jax
import jax.numpy as jnp
from jax import lax
from jax.sharding import PartitionSpec as P

PANEL = 512
NPAN = 2
highest = lax.Precision.HIGHEST


def from_root(value, axis, source):
    kept = jnp.where(lax.axis_index(axis) == source, value, 0).astype(value.dtype)
    return lax.psum(kept, axis)


def shards(
    tx_fields, rx_fields, layer_of_cell, layer_cond, tx_of_row, rx_of_row, damping, panel_order
):
    grp_count = lax.axis_size("grp")
    tile_count = lax.axis_size("tile")
    tile_cells = tx_fields.shape[1]
    total_rows = tx_of_row.shape[0]
    group_rows = total_rows // grp_count
    tile_cols = total_rows // tile_count
    group_start = lax.axis_index("grp") * group_rows
    tile_start = lax.axis_index("tile") * tile_cols
    levels = jnp.arange(layer_cond.shape[0], dtype=jnp.int32)
    layer_hot = (levels[:, None] == layer_of_cell[None, :]).astype(jnp.float32)
    cell_cond = jnp.dot(layer_cond[None, :], layer_hot, precision=highest)[0]
    contract = (((1,), (1,)), ((), ()))
    product = (
        jnp.take(
            tx_fields, lax.dynamic_slice_in_dim(tx_of_row, group_start, group_rows), axis=0
        ).astype(jnp.float32)
        * jnp.take(
            rx_fields, lax.dynamic_slice_in_dim(rx_of_row, group_start, group_rows), axis=0
        ).astype(jnp.float32)
        * cell_cond[None, :]
    )
    sens_own = product.astype(jnp.bfloat16)
    block_cols = lax.psum_scatter(
        lax.dot_general(
            lax.all_gather(sens_own, "grp", axis=0, tiled=True),
            sens_own,
            contract,
            preferred_element_type=jnp.float32,
        ),
        "tile",
        scatter_dimension=0,
        tiled=True,
    )
    cell_total = tile_cells * tile_count
    row_ids = group_start + jnp.arange(group_rows, dtype=jnp.int32)
    col_ids = tile_start + jnp.arange(tile_cols, dtype=jnp.int32)
    on_diagonal = row_ids[:, None] == col_ids[None, :]
    damp_rows = lax.dynamic_slice_in_dim(damping, group_start, group_rows)
    trailing = block_cols.T / cell_total + jnp.where(on_diagonal, damp_rows[:, None], 0.0)
    factor_parts = []
    for turn_index in range(NPAN):
        chosen = panel_order[turn_index * PANEL : (turn_index + 1) * PANEL]
        col_pick = (col_ids[:, None] == chosen[None, :]).astype(jnp.float32)
        row_pick = (chosen[:, None] == row_ids[None, :]).astype(jnp.float32)
        columns = lax.psum(jnp.dot(trailing, col_pick, precision=highest), "tile")
        diag_block = lax.psum(jnp.dot(row_pick, columns, precision=highest), "grp")
        block_factor = jnp.linalg.cholesky(diag_block)
        panel_factor = lax.linalg.triangular_solve(
            block_factor, columns, left_side=False, lower=True, transpose_a=True
        )
        owner_index = lax.axis_index("tile") * tile_cols // group_rows
        owned_rows = lax.dynamic_slice_in_dim(
            panel_factor, tile_start - owner_index * group_rows, tile_cols, 0
        )
        column_factor = from_root(owned_rows, "grp", owner_index)
        trailing = trailing - jnp.dot(panel_factor, column_factor.T, precision=highest)
        factor_parts.append(panel_factor)
    return (trailing, jnp.concatenate(factor_parts, axis=1))


def solution(mesh):
    placed = (P(None, "tile"), P(None, "tile"), P("tile"), P(), P(), P(), P(), P())
    return jax.shard_map(
        shards,
        mesh=mesh,
        in_specs=placed,
        out_specs=(P("grp", "tile"), P("grp", None)),
        check_vma=False,
    )
```

profile of v0, /device:TPU:8, one launch (start us, length us, event | category | flops | bytes accessed | tf_op | source)
XLA Modules:
  0.0 1140.9 jit_solution(2589747190513932107)
XLA Ops:
  7.2 0.8 compare_and_fusion
  8.1 3.7 gather_fusion
  11.9 2.1 gather_fusion.1
  14.2 1.2 multiply_convert_fusion
  15.5 44.2 %all-gather.2.cloned.1.call-done = bf16[2816,1024]{1,0:T(8,128)(2,1)} async-done(((bf16[352,1024]{1,0:T(8,128)(2,1)}), bf16[2816,1024]{1,0:T(8,128)(2,1)}) %all-gather.2.cloned.1.call-update) | async-done | bytes 5767184 | tf_op jit(solution)/shard_map/all_gather | solution.py:43
  59.6 8.0 fusion.89
  67.7 0.8 dynamic_slice.17
  68.5 0.8 fusion.88
  69.3 211.2 %reduce-scatter.4.cloned.1.call-done = f32[88,352]{1,0:T(8,128)} async-done(((f32[2816,352]{1,0:T(8,128)}), f32[88,352]{1,0:T(8,128)}) %reduce-scatter.4.cloned.1.call-update) | async-done | bytes 123920
  280.5 2.3 fusion.42
  282.9 149.3 %all-reduce.9.cloned.1.call-done = f32[352,512]{1,0:T(8,128)} async-done(((f32[352,512]{1,0:T(8,128)}), f32[352,512]{1,0:T(8,128)}) %all-reduce.9.cloned.1.call-update) | async-done | bytes 720912 | tf_op jit(solution)/shard_map/psum | solution.py:63
  432.2 3.2 fusion.4
  436.0 65.5 %all-reduce.11.cloned.1.call-done = f32[512,512]{0,1:T(8,128)} async-done(((f32[512,512]{0,1:T(8,128)}), f32[512,512]{0,1:T(8,128)}) %all-reduce.11.cloned.1.call-update) | async-done | bytes 1048592 | tf_op jit(solution)/shard_map/psum | solution.py:64
  501.5 1.6 copy.15
  503.4 11.7 %cholesky.286 = f32[128,128]{1,0:T(8,128)S(1)} custom-call(f32[128,128]{1,0:T(8,128)S(1)} %cholesky.426), custom_call_target="Cholesky" | custom-call | tf_op jit(solution)/shard_map/jit(cholesky)/cholesky | solution.py:65
  515.3 9.8 custom-call.27
  525.8 11.7 %cholesky.305 = f32[128,128]{1,0:T(8,128)S(1)} custom-call(f32[128,128]{1,0:T(8,128)S(1)} %cholesky.430), custom_call_target="Cholesky" | custom-call | tf_op jit(solution)/shard_map/jit(cholesky)/cholesky | solution.py:65
  537.5 0.7 compare_reduce_fusion.6
  538.8 10.0 custom-call.28
  549.5 11.7 %cholesky.326 = f32[128,128]{1,0:T(8,128)S(1)} custom-call(f32[128,128]{1,0:T(8,128)S(1)} %cholesky.435), custom_call_target="Cholesky" | custom-call | tf_op jit(solution)/shard_map/jit(cholesky)/cholesky | solution.py:65
  561.2 0.7 compare_reduce_fusion.5
  561.9 9.8 custom-call.29
  572.3 11.7 %cholesky.343 = f32[128,128]{1,0:T(8,128)S(1)} custom-call(f32[128,128]{1,0:T(8,128)S(1)} %convolution_subtract_fusion.13), custom_call_target="Cholesky" | custom-call | tf_op jit(solution)/shard_map/jit(cholesky)/cholesky | solution.py:65
  584.0 0.7 compare_reduce_fusion.4
  587.7 8.1 while.4
  588.4 1.4 bitcast_dynamic-update-slice_fusion.4
  590.4 1.4 bitcast_dynamic-update-slice_fusion.4
  592.4 1.4 bitcast_dynamic-update-slice_fusion.4
  594.4 1.4 bitcast_dynamic-update-slice_fusion.4
  595.8 39.3 %custom-call.30 = f32[4,128,128]{1,2,0:T(8,128)S(1)} custom-call(f32[4,128,128]{2,1,0:T(8,128)S(1)} %get-tuple-element.18), custom_call_target="InvertDiagBlocksLowerTriangular" | custom-call | tf_op jit(solution)/shard_map/triangular_solve/custom-call.3 | solution.py:66
  637.8 0.7 dynamic-slice_select_fusion.1
  638.6 64.7 %all-reduce.13.cloned.1.call-done = f32[88,512]{1,0:T(8,128)} async-done(((f32[88,512]{1,0:T(8,128)}), f32[88,512]{1,0:T(8,128)}) %all-reduce.13.cloned.1.call-update) | async-done | bytes 180240 | tf_op jit(solution)/shard_map/psum | solution.py:13
  703.3 1.7 convolution_subtract_fusion.9
  705.0 1.4 fusion.40
  706.5 148.2 %all-reduce.15.cloned.1.call-done = f32[352,512]{1,0:T(8,128)} async-done(((f32[352,512]{1,0:T(8,128)}), f32[352,512]{1,0:T(8,128)}) %all-reduce.15.cloned.1.call-update) | async-done | bytes 720912 | tf_op jit(solution)/shard_map/psum | solution.py:63
  854.6 3.2 fusion.2
  858.3 65.5 %all-reduce.17.cloned.1.call-done = f32[512,512]{0,1:T(8,128)} async-done(((f32[512,512]{0,1:T(8,128)}), f32[512,512]{0,1:T(8,128)}) %all-reduce.17.cloned.1.call-update) | async-done | bytes 1048592 | tf_op jit(solution)/shard_map/psum | solution.py:64
  923.9 1.6 copy.17
  925.8 1.0 copy-done.7
  926.8 11.7 %cholesky.358 = f32[128,128]{1,0:T(8,128)S(1)} custom-call(f32[128,128]{1,0:T(8,128)S(1)} %cholesky.439), custom_call_target="Cholesky" | custom-call | tf_op jit(solution)/shard_map/jit(cholesky)/cholesky | solution.py:65
  938.6 9.8 custom-call.31
  948.5 1.2 constant_dynamic-update-slice_fusion.3
  949.7 1.3 convolution_subtract_fusion
  951.0 11.7 %cholesky.377 = f32[128,128]{1,0:T(8,128)S(1)} custom-call(f32[128,128]{1,0:T(8,128)S(1)} %cholesky.443), custom_call_target="Cholesky" | custom-call | tf_op jit(solution)/shard_map/jit(cholesky)/cholesky | solution.py:65
  963.4 0.7 compare_reduce_fusion.3
  964.1 9.9 custom-call.32
  974.3 1.3 convolution_subtract_fusion.10
  975.6 11.7 %cholesky.398 = f32[128,128]{1,0:T(8,128)S(1)} custom-call(f32[128,128]{1,0:T(8,128)S(1)} %cholesky.448), custom_call_target="Cholesky" | custom-call | tf_op jit(solution)/shard_map/jit(cholesky)/cholesky | solution.py:65
  987.4 0.7 compare_reduce_fusion.1
  988.0 9.8 custom-call.33
  998.1 1.2 convolution_subtract_fusion.12
  999.3 11.7 %cholesky.415 = f32[128,128]{1,0:T(8,128)S(1)} custom-call(f32[128,128]{1,0:T(8,128)S(1)} %convolution_subtract_fusion.12), custom_call_target="Cholesky" | custom-call | tf_op jit(solution)/shard_map/jit(cholesky)/cholesky | solution.py:65
  1011.0 0.6 compare_reduce_fusion
  1014.6 8.5 while.5
  1015.3 1.4 bitcast_dynamic-update-slice_fusion.5
  1017.4 1.4 bitcast_dynamic-update-slice_fusion.5
  1019.5 1.4 bitcast_dynamic-update-slice_fusion.5
  1021.6 1.4 bitcast_dynamic-update-slice_fusion.5
  1023.1 39.3 %custom-call.34 = f32[4,128,128]{1,2,0:T(8,128)S(1)} custom-call(f32[4,128,128]{2,1,0:T(8,128)S(1)} %get-tuple-element.19), custom_call_target="InvertDiagBlocksLowerTriangular" | custom-call | tf_op jit(solution)/shard_map/triangular_solve/custom-call.3 | solution.py:66
  1064.8 1.2 fusion.60
  1066.0 0.7 dynamic-slice_select_fusion
  1066.8 1.2 maximum_maximum_fusion
  1068.0 63.6 %all-reduce.19.cloned.1.call-done = f32[88,512]{1,0:T(8,128)} async-done(((f32[88,512]{1,0:T(8,128)}), f32[88,512]{1,0:T(8,128)}) %all-reduce.19.cloned.1.call-update) | async-done | bytes 180240 | tf_op jit(solution)/shard_map/psum | solution.py:13
  1131.5 2.3 convolution_subtract_fusion.8
  (117 shorter events, 17.0 us)
Async XLA Ops:
  7.2 4.7 copy-start
  7.2 52.5 %all-gather.2.cloned.1.call-start = ((), (), s32[]{:S(2)}) async-start(), calls=%async_computation.1 | async-start | bytes 6488064 | tf_op jit(solution)/shard_map/all_gather | solution.py:43
  11.8 2.1 copy-start.14
  11.8 2.1 copy-start.15
  15.4 265.0 %reduce-scatter.4.cloned.1.call-start = ((), (), s32[]{:S(2)}) async-start(), calls=%async_computation.8 | async-start | bytes 4460544
  67.7 364.5 %all-reduce.9.cloned.1.call-start = ((), (), s32[]{:S(2)}) async-start(), calls=%async_computation.2 | async-start | bytes 1441792 | tf_op jit(solution)/shard_map/psum | solution.py:63
  282.8 218.7 %all-reduce.11.cloned.1.call-start = ((), (), s32[]{:S(2)}) async-start(), calls=%async_computation.3 | async-start | bytes 2097152 | tf_op jit(solution)/shard_map/psum | solution.py:64
  435.5 267.9 %all-reduce.13.cloned.1.call-start = ((), (), s32[]{:S(2)}) async-start(), calls=%async_computation.4 | async-start | bytes 360448 | tf_op jit(solution)/shard_map/psum | solution.py:13
  501.5 1.7 copy-start.1
  587.4 47.8 %copy-start.3 = (f32[352,512]{1,0:T(8,128)S(1)}, f32[352,512]{1,0:T(8,128)}, u32[]{:S(2)}) copy-start(f32[352,512]{1,0:T(8,128)} %all-reduce.9.cloned.1.call-done) | copy-start | bytes 2162692
  636.8 66.5 %copy-start.5 = (f32[352,128]{1,0:T(8,128)}, f32[352,128]{1,0:T(8,128)S(1)}, u32[]{:S(2)}) copy-start(f32[352,128]{1,0:T(8,128)S(1)} %fusion.67) | copy-start | bytes 540676
  637.4 65.9 %copy-start.11 = (f32[88,352]{1,0:T(8,128)S(1)}, f32[88,352]{1,0:T(8,128)}, u32[]{:S(2)}) copy-start(f32[88,352]{1,0:T(8,128)} %reduce-scatter.4.cloned.1.call-done) | copy-start | bytes 371716
  637.8 67.2 %copy-start.8 = (f32[352,128]{1,0:T(8,128)}, f32[352,128]{1,0:T(8,128)S(1)}, u32[]{:S(2)}) copy-start(f32[352,128]{1,0:T(8,128)S(1)} %fusion.66) | copy-start | bytes 540676
  638.6 216.1 %all-reduce.15.cloned.1.call-start = ((), (), s32[]{:S(2)}) async-start(), calls=%async_computation.5 | async-start | bytes 1441792 | tf_op jit(solution)/shard_map/psum | solution.py:63
  705.0 152.9 %copy-start.12 = (f32[352,88]{0,1:T(8,128)}, f32[352,88]{0,1:T(8,128)S(1)}, u32[]{:S(2)}) copy-start(f32[352,88]{0,1:T(8,128)S(1)} %convolution_subtract_fusion.9) | copy-start | bytes 371716
  706.4 217.5 %all-reduce.17.cloned.1.call-start = ((), (), s32[]{:S(2)}) async-start(), calls=%async_computation.6 | async-start | bytes 2097152 | tf_op jit(solution)/shard_map/psum | solution.py:64
  857.9 273.6 %all-reduce.19.cloned.1.call-start = ((), (), s32[]{:S(2)}) async-start(), calls=%async_computation.7 | async-start | bytes 360448 | tf_op jit(solution)/shard_map/psum | solution.py:13
  923.9 1.7 copy-start.2
  925.8 1.0 copy-start.7
  1014.2 48.2 %copy-start.4 = (f32[352,512]{1,0:T(8,128)S(1)}, f32[352,512]{1,0:T(8,128)}, u32[]{:S(2)}) copy-start(f32[352,512]{1,0:T(8,128)} %all-reduce.15.cloned.1.call-done) | copy-start | bytes 2162692
  1062.4 1.7 copy-start.10
  1064.7 2.0 copy-start.6
  1064.7 2.0 copy-start.9
  1066.7 64.8 %copy-start.13 = (f32[352,88]{0,1:T(8,128)S(1)}, f32[352,88]{0,1:T(8,128)}, u32[]{:S(2)}) copy-start(f32[352,88]{0,1:T(8,128)} %copy-done.12) | copy-start | bytes 371716
Sparse Core Ops, SparseCore 0:
  15.6 44.0 all-gather.1
  67.8 212.6 reduce-scatter.3
  284.4 147.7 all-reduce.8
  435.6 65.8 all-reduce.10
  638.7 64.6 all-reduce.12
  707.2 147.4 all-reduce.14
  858.0 65.8 all-reduce.16
  1066.8 64.6 all-reduce.18
where the time goes:
time: 1150 us; the launch traced here: 1140 us
  waiting for transfers between devices  812 us (71%)
  other arithmetic  243 us (21%)
  matrix products  35.7 us (3%)
  local copies, waits for them, and re-layouts  28.4 us (2%)
  between operations  20.2 us (2%)
    psum x2, waiting for transfers between devices, shards(): columns = lax.psum(jnp.dot(trailing, col_pick, precision=highest), 'tile')  298 us
    unnamed x9, waiting for transfers between devices  211 us
    another operation x30, other arithmetic, shards(): block_factor = jnp.linalg.cholesky(diag_block)  158 us
    psum x2, waiting for transfers between devices, shards(): diag_block = lax.psum(jnp.dot(row_pick, columns, precision=highest), 'grp')  131 us
    psum x2, waiting for transfers between devices, from_root(): return lax.psum(kept, axis)  128 us
    another operation x7, other arithmetic, shards(): lax.linalg.triangular_solve(block_factor, columns, left_side=False, lower...  79.4 us
    all_gather x1, waiting for transfers between devices, shards(): lax.all_gather(sens_own, 'grp', axis=0, tiled=True)  44.2 us
  transfers between devices with their start and end apart: 8, of which 8 were waited for; matrix products, arithmetic and copies ran while one was open for 0% of the time, Pallas kernels for 0%

commit v1 on v0

--- a/solution.py
+++ b/solution.py
@@ -60,7 +60,9 @@
         chosen = panel_order[turn_index * PANEL : (turn_index + 1) * PANEL]
         col_pick = (col_ids[:, None] == chosen[None, :]).astype(jnp.float32)
         row_pick = (chosen[:, None] == row_ids[None, :]).astype(jnp.float32)
-        columns = lax.psum(jnp.dot(trailing, col_pick, precision=highest), "tile")
+        columns = jnp.sum(
+            lax.all_gather(jnp.dot(trailing, col_pick, precision=highest), "tile"), axis=0
+        )
         diag_block = lax.psum(jnp.dot(row_pick, columns, precision=highest), "grp")
         block_factor = jnp.linalg.cholesky(diag_block)
         panel_factor = lax.linalg.triangular_solve(

time: 1150 us -> 1210 us (1.052)
  waiting for transfers between devices: 812 us -> 855 us
  other arithmetic: 243 us -> 260 us
    all_gather x0 -> x2, waiting for transfers between devices: none -> 340 us  [shards(): lax.all_gather(jnp.dot(trailing, col_pick, precision=highest), 'tile')]
    psum x2 -> x0, waiting for transfers between devices: 298 us -> none  [shards(): columns = lax.psum(jnp.dot(trailing, col_pick, precision=highest), 'tile')]
    reduce_sum x0 -> x2, other arithmetic: none -> 17.5 us  [shards(): jnp.sum(lax.all_gather(jnp.dot(trailing, col_pick, precision=highest), 't...]
where the time goes in v1:
time: 1210 us; the launch traced here: 1200 us
  waiting for transfers between devices  855 us (71%)
  other arithmetic  260 us (21%)
  matrix products  36.2 us (3%)
  local copies, waits for them, and re-layouts  30.4 us (3%)
  between operations  20 us (2%)
    all_gather x2, waiting for transfers between devices, shards(): lax.all_gather(jnp.dot(trailing, col_pick, precision=highest), 'tile')  340 us
    unnamed x9, waiting for transfers between devices  211 us
    another operation x30, other arithmetic, shards(): block_factor = jnp.linalg.cholesky(diag_block)  158 us
    psum x2, waiting for transfers between devices, shards(): diag_block = lax.psum(jnp.dot(row_pick, columns, precision=highest), 'grp')  131 us
    psum x2, waiting for transfers between devices, from_root(): return lax.psum(kept, axis)  128 us
    another operation x7, other arithmetic, shards(): lax.linalg.triangular_solve(block_factor, columns, left_side=False, lower...  79.4 us
    all_gather x1, waiting for transfers between devices, shards(): lax.all_gather(sens_own, 'grp', axis=0, tiled=True)  44.2 us
  transfers between devices with their start and end apart: 8, of which 8 were waited for; matrix products, arithmetic and copies ran while one was open for 0% of the time, Pallas kernels for 0%

profile of v1, /device:TPU:8, one launch (start us, length us, event | category | flops | bytes accessed | tf_op | source)
XLA Modules:
  0.0 1203.5 jit_solution(5412205346314511483)
XLA Ops:
  7.2 0.8 compare_and_fusion
  8.1 3.7 gather_fusion
  11.9 2.1 gather_fusion.1
  14.2 1.2 multiply_convert_fusion
  15.5 44.2 %all-gather.6.cloned.1.call-done = bf16[2816,1024]{1,0:T(8,128)(2,1)} async-done(((bf16[352,1024]{1,0:T(8,128)(2,1)}), bf16[2816,1024]{1,0:T(8,128)(2,1)}) %all-gather.6.cloned.1.call-update) | async-done | bytes 5767184 | tf_op jit(solution)/shard_map/all_gather | solution.py:43
  59.6 8.0 fusion.89
  67.8 0.8 dynamic_slice.17
  68.5 0.8 fusion.88
  69.3 211.2 %reduce-scatter.4.cloned.1.call-done = f32[88,352]{1,0:T(8,128)} async-done(((f32[2816,352]{1,0:T(8,128)}), f32[88,352]{1,0:T(8,128)}) %reduce-scatter.4.cloned.1.call-update) | async-done | bytes 123920
  280.5 2.3 fusion.42
  282.9 170.4 %all-gather.8.cloned.1.call-done = f32[11264,512]{1,0:T(8,128)} async-done(((f32[352,512]{1,0:T(8,128)}), f32[11264,512]{1,0:T(8,128)}) %all-gather.8.cloned.1.call-update) | async-done | bytes 23068688 | tf_op jit(solution)/shard_map/all_gather | solution.py:64
  453.2 8.7 reduce_sum.18
  462.0 2.1 fusion.4
  464.7 65.7 %all-reduce.7.cloned.1.call-done = f32[512,512]{0,1:T(8,128)} async-done(((f32[512,512]{0,1:T(8,128)}), f32[512,512]{0,1:T(8,128)}) %all-reduce.7.cloned.1.call-update) | async-done | bytes 1048592 | tf_op jit(solution)/shard_map/psum | solution.py:66
  530.4 1.6 copy.15
  532.3 1.0 copy-done.6
  533.2 11.7 cholesky.286
  545.1 9.8 custom-call.27
  554.9 1.2 constant_dynamic-update-slice_fusion.5
  556.2 1.3 convolution_subtract_fusion.1
  557.5 11.7 cholesky.305
  569.8 0.7 compare_reduce_fusion.7
  570.6 10.0 custom-call.28
  580.8 1.3 convolution_subtract_fusion.11
  582.1 11.7 cholesky.326
  594.5 9.8 custom-call.29
  604.5 1.2 convolution_subtract_fusion.13
  605.8 11.7 cholesky.343
  621.1 8.5 while.4
  621.8 1.4 bitcast_dynamic-update-slice_fusion.4
  623.9 1.4 bitcast_dynamic-update-slice_fusion.4
  626.0 1.4 bitcast_dynamic-update-slice_fusion.4
  628.1 1.4 bitcast_dynamic-update-slice_fusion.4
  629.6 39.3 %custom-call.30 = f32[4,128,128]{1,2,0:T(8,128)S(1)} custom-call(f32[4,128,128]{2,1,0:T(8,128)S(1)} %get-tuple-element.18), custom_call_target="InvertDiagBlocksLowerTriangular" | custom-call | tf_op jit(solution)/shard_map/triangular_solve/custom-call.3 | solution.py:68
  672.4 64.8 %all-reduce.9.cloned.1.call-done = f32[88,512]{1,0:T(8,128)} async-done(((f32[88,512]{1,0:T(8,128)}), f32[88,512]{1,0:T(8,128)}) %all-reduce.9.cloned.1.call-update) | async-done | bytes 180240 | tf_op jit(solution)/shard_map/psum | solution.py:13
  737.2 1.7 convolution_subtract_fusion.9
  739.5 1.4 fusion.40
  741.0 169.4 %all-gather.10.cloned.1.call-done = f32[11264,512]{1,0:T(8,128)} async-done(((f32[352,512]{1,0:T(8,128)}), f32[11264,512]{1,0:T(8,128)}) %all-gather.10.cloned.1.call-update) | async-done | bytes 23068688 | tf_op jit(solution)/shard_map/all_gather | solution.py:64
  910.4 8.7 reduce_sum.19
  919.1 2.1 fusion.2
  921.7 65.7 %all-reduce.11.cloned.1.call-done = f32[512,512]{0,1:T(8,128)} async-done(((f32[512,512]{0,1:T(8,128)}), f32[512,512]{0,1:T(8,128)}) %all-reduce.11.cloned.1.call-update) | async-done | bytes 1048592 | tf_op jit(solution)/shard_map/psum | solution.py:66
  987.4 1.6 copy.17
  989.4 1.0 copy-done.7
  990.3 11.7 cholesky.358
  1002.2 9.8 custom-call.31
  1012.0 1.2 constant_dynamic-update-slice_fusion.3
  1013.3 1.3 convolution_subtract_fusion
  1014.5 11.7 cholesky.377
  1026.9 0.7 compare_reduce_fusion.3
  1027.6 9.9 custom-call.32
  1037.9 1.3 convolution_subtract_fusion.10
  1039.2 11.7 cholesky.398
  1051.5 9.8 custom-call.33
  1061.6 1.2 convolution_subtract_fusion.12
  1062.8 11.7 cholesky.415
  1078.0 8.5 while.5
  1078.7 1.4 bitcast_dynamic-update-slice_fusion.5
  1080.8 1.4 bitcast_dynamic-update-slice_fusion.5
  1082.9 1.4 bitcast_dynamic-update-slice_fusion.5
  1085.1 1.4 bitcast_dynamic-update-slice_fusion.5
  1086.5 39.3 %custom-call.34 = f32[4,128,128]{1,2,0:T(8,128)S(1)} custom-call(f32[4,128,128]{2,1,0:T(8,128)S(1)} %get-tuple-element.19), custom_call_target="InvertDiagBlocksLowerTriangular" | custom-call | tf_op jit(solution)/shard_map/triangular_solve/custom-call.3 | solution.py:68
  1129.3 1.2 maximum_maximum_fusion
  1130.5 63.6 %all-reduce.13.cloned.1.call-done = f32[88,512]{1,0:T(8,128)} async-done(((f32[88,512]{1,0:T(8,128)}), f32[88,512]{1,0:T(8,128)}) %all-reduce.13.cloned.1.call-update) | async-done | bytes 180240 | tf_op jit(solution)/shard_map/psum | solution.py:13
  1194.1 2.3 convolution_subtract_fusion.8
  (117 shorter events, 20.7 us)
Async XLA Ops:
  7.2 4.7 copy-start
  7.2 52.5 %all-gather.6.cloned.1.call-start = ((), (), s32[]{:S(2)}) async-start(), calls=%async_computation.1 | async-start | bytes 6488064 | tf_op jit(solution)/shard_map/all_gather | solution.py:43
  11.8 2.1 copy-start.13
  11.9 2.1 copy-start.14
  15.4 265.0 %reduce-scatter.4.cloned.1.call-start = ((), (), s32[]{:S(2)}) async-start(), calls=%async_computation.8 | async-start | bytes 4460544
  67.7 385.5 %all-gather.8.cloned.1.call-start = ((), (), s32[]{:S(2)}) async-start(), calls=%async_computation.6 | async-start | bytes 23789568 | tf_op jit(solution)/shard_map/all_gather | solution.py:64
  282.8 247.5 %all-reduce.7.cloned.1.call-start = ((), (), s32[]{:S(2)}) async-start(), calls=%async_computation.2 | async-start | bytes 2097152 | tf_op jit(solution)/shard_map/psum | solution.py:66
  464.1 273.1 %all-reduce.9.cloned.1.call-start = ((), (), s32[]{:S(2)}) async-start(), calls=%async_computation.3 | async-start | bytes 360448 | tf_op jit(solution)/shard_map/psum | solution.py:13
  530.4 1.7 copy-start.2
  532.3 1.0 copy-start.6
  670.6 66.6 %copy-start.4 = (f32[352,128]{1,0:T(8,128)}, f32[352,128]{1,0:T(8,128)S(1)}, u32[]{:S(2)}) copy-start(f32[352,128]{1,0:T(8,128)S(1)} %fusion.67) | copy-start | bytes 540676
  671.2 66.0 %copy-start.10 = (f32[88,352]{1,0:T(8,128)S(1)}, f32[88,352]{1,0:T(8,128)}, u32[]{:S(2)}) copy-start(f32[88,352]{1,0:T(8,128)} %reduce-scatter.4.cloned.1.call-done) | copy-start | bytes 371716
  671.5 67.3 %copy-start.8 = (f32[352,128]{1,0:T(8,128)}, f32[352,128]{1,0:T(8,128)S(1)}, u32[]{:S(2)}) copy-start(f32[352,128]{1,0:T(8,128)S(1)} %fusion.66) | copy-start | bytes 540676
  672.3 238.1 %all-gather.10.cloned.1.call-start = ((), (), s32[]{:S(2)}) async-start(), calls=%async_computation.7 | async-start | bytes 23789568 | tf_op jit(solution)/shard_map/all_gather | solution.py:64
  738.9 0.7 copy-start.11
  740.9 246.5 %all-reduce.11.cloned.1.call-start = ((), (), s32[]{:S(2)}) async-start(), calls=%async_computation.4 | async-start | bytes 2097152 | tf_op jit(solution)/shard_map/psum | solution.py:66
  921.3 272.8 %all-reduce.13.cloned.1.call-start = ((), (), s32[]{:S(2)}) async-start(), calls=%async_computation.5 | async-start | bytes 360448 | tf_op jit(solution)/shard_map/psum | solution.py:13
  987.4 1.7 copy-start.3
  989.3 1.0 copy-start.7
  1128.1 1.1 copy-start.5
  1128.2 1.1 copy-start.9
  1129.3 64.9 %copy-start.12 = (f32[352,88]{0,1:T(8,128)S(1)}, f32[352,88]{0,1:T(8,128)}, u32[]{:S(2)}) copy-start(f32[352,88]{0,1:T(8,128)} %copy-done.11) | copy-start | bytes 371716
  1129.3 67.2 %copy-start.1 = (bf16[128,1024]{1,0:T(8,128)(2,1)S(1)}, bf16[128,1024]{1,0:T(8,128)(2,1)}, u32[]{:S(2)}) copy-start(bf16[128,1024]{1,0:T(8,128)(2,1)} %param.12) | copy-start | bytes 786436
Sparse Core Ops, SparseCore 0:
  15.6 44.0 all-gather.5
  67.8 212.5 reduce-scatter.3
  283.6 169.5 all-gather.7
  464.2 66.0 all-reduce.6
  672.4 64.7 all-reduce.8
  741.0 169.3 all-gather.9
  921.4 65.9 all-reduce.10
  1129.4 64.7 all-reduce.12
